TPU v7x, 128 devices: a whole 4x4x4 slice. The times are simulated.
128 devices in a mesh: dp: 4 (over x), grid: 32 (over z, y, core).
Axes of the slice: x: 4, y: 4, z: 4, core: 2. Of those that a mesh axis runs over, the one named last changes fastest.
Arguments:
- intensities: bfloat16 [8192, 32, 128], P(('dp', 'grid')), may hold values from -6 to 6
- gridding: bfloat16 [8192, 32, 512], P(('dp', 'grid')), may hold values from -0.0625 to 0.0625
- dest_slab: int32 [8192, 1], P(('dp', 'grid')), may hold values from 0 to 31; in each aligned block of 64 rows (0 to 63, 64 to 127, ...) at most 4 rows name the same one
- spectral_weights: float32 [4, 128, 128, 128], P('dp', None, 'grid'), may hold values from 0.05 to 2
Outputs:
- solution_field: float32 [128, 128, 128], P('grid')
- residual: float32 [128, 128, 128], P('grid')
Inputs may be any that keep to these rules, and one draw needn't show every extreme that they name: `dest_slab`: at most 4 of one device's 64 snapshots name the same slab, and in every draw some device has exactly 4 that name one slab.
All inputs are finite; a program needn't handle non-finite values.
Results may differ from a plain program's by a relative error of at most 0.0003.
Values may be sent and summed in bfloat16 or wider, within the bound.
No kernel may reach another device: no remote copies, remote signals or barrier semaphores. Data moves between devices by JAX's collectives and lax.ppermute only.
A program may use at most 128 MiB of HBM per device.

v0:
```python
import math

import jax
import jax.numpy as jnp
from jax import lax
from jax.sharding import PartitionSpec as P

ITERS = 8


def tables(size):
    index = jnp.arange(size, dtype=jnp.int32)
    phase = index[:, None] * index[None, :] % size
    angle = phase.astype(jnp.float32) * (2.0 * math.pi / size)
    return (jnp.cos(angle), jnp.sin(angle))


def along(form, field, table):
    return jnp.einsum(form, field, table, precision=lax.Precision.HIGHEST)


def rotate(form, real_part, imag_part, cos_table, sin_table, sign):
    new_real = along(form, real_part, cos_table) - sign * along(form, imag_part, sin_table)
    new_imag = along(form, imag_part, cos_table) + sign * along(form, real_part, sin_table)
    return (new_real, new_imag)


def operate_slabs(field, weights, cos_table, sin_table):
    size = field.shape[1]
    first_real = along("ayz,zk->ayk", field, cos_table)
    first_imag = -along("ayz,zk->ayk", field, sin_table)
    mid_real, mid_imag = rotate("ayz,yk->akz", first_real, first_imag, cos_table, sin_table, -1.0)
    col_real, col_imag = (
        lax.all_to_all(mid_real, "grid", split_axis=1, concat_axis=0, tiled=True),
        lax.all_to_all(mid_imag, "grid", split_axis=1, concat_axis=0, tiled=True),
    )
    spec_real, spec_imag = rotate("ayz,ak->kyz", col_real, col_imag, cos_table, sin_table, -1.0)
    back_real, back_imag = rotate(
        "ayz,ak->kyz", weights * spec_real, weights * spec_imag, cos_table, sin_table, 1.0
    )
    plane_real, plane_imag = (
        lax.all_to_all(back_real, "grid", split_axis=0, concat_axis=1, tiled=True),
        lax.all_to_all(back_imag, "grid", split_axis=0, concat_axis=1, tiled=True),
    )
    row_real, row_imag = rotate("ayz,yk->akz", plane_real, plane_imag, cos_table, sin_table, 1.0)
    result = along("ayz,zk->ayk", row_real, cos_table) - along("ayz,zk->ayk", row_imag, sin_table)
    return result * (1.0 / (size * size * size))


def body(intensities, gridding, dest_slab, spectral_weights):
    ngrid = lax.axis_size("grid")
    ndp = lax.axis_size("dp")
    nent, rows, size = intensities.shape
    slab_rows = gridding.shape[2]
    planes = slab_rows // size
    capacity = max(2, 2 * nent // ngrid)
    target = dest_slab[:, 0]
    member = (target[:, None] == jnp.arange(ngrid, dtype=jnp.int32)[None, :]).astype(jnp.int32)
    before = jnp.sum((jnp.cumsum(member, axis=0) - member) * member, axis=1)
    slot = target * capacity + before
    value_slots = (
        jnp.zeros((ngrid * capacity, rows, size), intensities.dtype).at[slot].set(intensities)
    )
    matrix_slots = (
        jnp.zeros((ngrid * capacity, rows, slab_rows), gridding.dtype).at[slot].set(gridding)
    )
    value_dest = value_slots.reshape(ngrid, capacity * rows, size)
    matrix_dest = matrix_slots.reshape(ngrid, capacity * rows, slab_rows)
    product = lax.dot_general(
        matrix_dest, value_dest, (((1,), (1,)), ((0,), (0,))), preferred_element_type=jnp.float32
    )
    partial_value = lax.psum_scatter(
        product.reshape(slab_rows * lax.axis_size("grid"), size),
        "grid",
        scatter_dimension=0,
        tiled=True,
    )
    cos_table, sin_table = tables(size)
    quarter = size // ndp
    right_side = lax.psum(partial_value, "dp").reshape(planes, size, size)
    weights = lax.psum(spectral_weights[0], "dp")

    def own_rows(field):
        return lax.dynamic_slice_in_dim(field, lax.axis_index("dp") * quarter, quarter, 1)

    def squares(residual):
        part = own_rows(residual)
        return lax.psum(jnp.sum(part * part), ("dp", "grid"))

    solution_field = jnp.zeros_like(right_side)
    residual = right_side
    direction = right_side
    norm_now = squares(residual)
    for step in range(ITERS):
        image = operate_slabs(direction, weights, cos_table, sin_table)
        alpha = norm_now / lax.psum(jnp.sum(own_rows(direction) * own_rows(image)), ("dp", "grid"))
        solution_field = solution_field + alpha * direction
        residual = residual - alpha * image
        norm_next = squares(residual)
        direction = residual + norm_next / norm_now * direction
        norm_now = norm_next
    return (solution_field, residual)


def solution(mesh):
    return jax.shard_map(
        body,
        mesh=mesh,
        in_specs=(
            P(("dp", "grid"), None, None),
            P(("dp", "grid"), None, None),
            P(("dp", "grid"), None),
            P("dp", None, "grid", None),
        ),
        out_specs=(P("grid", None, None), P("grid", None, None)),
        check_vma=False,
    )
```

profile of v0, /device:TPU:1, one launch (start us, length us, event | category | flops | bytes accessed | tf_op | source)
XLA Modules:
  0.0 1668.7 jit_solution(5425736892697403691)
XLA Ops:
  12.2 8.7 scatter_fusion
  34.5 92.9 %reduce-scatter.2.cloned.1.call-done = f32[512,128]{1,0:T(8,128)} async-done(((f32[16384,128]{1,0:T(8,128)}), f32[512,128]{1,0:T(8,128)}) %reduce-scatter.2.cloned.1.call-update) | async-done | bytes 262160 | tf_op jit(solution)/shard_map/reduce_scatter | solution.py:72
  127.4 44.8 %all-reduce.4.cloned.1.call-done = (f32[4,128,128]{2,1,0:T(8,128)}, f32[128,4,128]{2,0,1:T(8,128)}) async-done(((f32[4,128,128]{2,1,0:T(8,128)}, f32[128,4,128]{2,0,1:T(8,128)}), (f32[4,128,128]{2,1,0:T(8,128)}, f32[128,4,128]{2,0,1:T(8,128)})) %all-reduce.4.cloned.1.call-update) | async-done | bytes 524304 | tf_op jit(solution)/shard_map/psum | solution.py:80
  177.6 9.9 all-to-all-start.1
  242.8 63.2 %all-reduce = (f32[]{:T(128)}, f32[]{:T(128)}) all-reduce(f32[]{:T(128)} %get-tuple-element.3, f32[]{:T(128)} %get-tuple-element.2), channel_id=1, replica_groups=mesh['dp'=4,'grid'=32] {'dp','grid'}, use_global_device_ids=true, to_apply=%region_7.8 | all-reduce | flops 2 | bytes 16 | tf_op jit(solution)/shard_map/psum | solution.py:88
  308.0 62.9 %psum.130 = f32[]{:T(128)} all-reduce(f32[]{:T(128)} %multiply_reduce_fusion.6), channel_id=1, replica_groups=mesh['dp'=4,'grid'=32] {'dp','grid'}, use_global_device_ids=true, to_apply=%region_12.13 | all-reduce | flops 1 | bytes 8 | tf_op jit(solution)/shard_map/psum | solution.py:88
  394.3 8.2 all-to-all-done.4
  423.9 8.2 all-to-all-done.6
  436.0 63.2 %psum.131 = f32[]{:T(128)} all-reduce(f32[]{:T(128)} %fusion.96), channel_id=1, replica_groups=mesh['dp'=4,'grid'=32] {'dp','grid'}, use_global_device_ids=true, to_apply=%region_14.15 | all-reduce | flops 1 | bytes 8 | tf_op jit(solution)/shard_map/psum | solution.py:96
  501.1 62.9 %psum.132 = f32[]{:T(128)} all-reduce(f32[]{:T(128)} %multiply_reduce_fusion.5), channel_id=1, replica_groups=mesh['dp'=4,'grid'=32] {'dp','grid'}, use_global_device_ids=true, to_apply=%region_16.17 | all-reduce | flops 1 | bytes 8 | tf_op jit(solution)/shard_map/psum | solution.py:88
  616.9 8.2 all-to-all-done.10
  629.0 63.0 %psum.133 = f32[]{:T(128)} all-reduce(f32[]{:T(128)} %fusion.94), channel_id=1, replica_groups=mesh['dp'=4,'grid'=32] {'dp','grid'}, use_global_device_ids=true, to_apply=%region_18.19 | all-reduce | flops 1 | bytes 8 | tf_op jit(solution)/shard_map/psum | solution.py:96
  694.1 62.9 %psum.134 = f32[]{:T(128)} all-reduce(f32[]{:T(128)} %multiply_reduce_fusion.4), channel_id=1, replica_groups=mesh['dp'=4,'grid'=32] {'dp','grid'}, use_global_device_ids=true, to_apply=%region_20.21 | all-reduce | flops 1 | bytes 8 | tf_op jit(solution)/shard_map/psum | solution.py:88
  780.5 8.2 all-to-all-done.12
  822.2 63.0 %psum.135 = f32[]{:T(128)} all-reduce(f32[]{:T(128)} %fusion.92), channel_id=1, replica_groups=mesh['dp'=4,'grid'=32] {'dp','grid'}, use_global_device_ids=true, to_apply=%region_22.23 | all-reduce | flops 1 | bytes 8 | tf_op jit(solution)/shard_map/psum | solution.py:96
  887.1 63.1 %psum.136 = f32[]{:T(128)} all-reduce(f32[]{:T(128)} %multiply_reduce_fusion.3), channel_id=1, replica_groups=mesh['dp'=4,'grid'=32] {'dp','grid'}, use_global_device_ids=true, to_apply=%region_24.25 | all-reduce | flops 1 | bytes 8 | tf_op jit(solution)/shard_map/psum | solution.py:88
  1015.2 63.0 %psum.137 = f32[]{:T(128)} all-reduce(f32[]{:T(128)} %fusion.90), channel_id=1, replica_groups=mesh['dp'=4,'grid'=32] {'dp','grid'}, use_global_device_ids=true, to_apply=%region_26.27 | all-reduce | flops 1 | bytes 8 | tf_op jit(solution)/shard_map/psum | solution.py:96
  1080.3 62.9 %psum.138 = f32[]{:T(128)} all-reduce(f32[]{:T(128)} %multiply_reduce_fusion.2), channel_id=1, replica_groups=mesh['dp'=4,'grid'=32] {'dp','grid'}, use_global_device_ids=true, to_apply=%region_28.29 | all-reduce | flops 1 | bytes 8 | tf_op jit(solution)/shard_map/psum | solution.py:88
  1196.3 8.2 all-to-all-done.22
  1208.4 63.0 %psum.139 = f32[]{:T(128)} all-reduce(f32[]{:T(128)} %fusion.88), channel_id=1, replica_groups=mesh['dp'=4,'grid'=32] {'dp','grid'}, use_global_device_ids=true, to_apply=%region_30.31 | all-reduce | flops 1 | bytes 8 | tf_op jit(solution)/shard_map/psum | solution.py:96
  1273.3 63.1 %psum.140 = f32[]{:T(128)} all-reduce(f32[]{:T(128)} %multiply_reduce_fusion.1), channel_id=1, replica_groups=mesh['dp'=4,'grid'=32] {'dp','grid'}, use_global_device_ids=true, to_apply=%region_32.33 | all-reduce | flops 1 | bytes 8 | tf_op jit(solution)/shard_map/psum | solution.py:88
  1401.4 63.0 %psum.141 = f32[]{:T(128)} all-reduce(f32[]{:T(128)} %fusion.86), channel_id=1, replica_groups=mesh['dp'=4,'grid'=32] {'dp','grid'}, use_global_device_ids=true, to_apply=%region_34.35 | all-reduce | flops 1 | bytes 8 | tf_op jit(solution)/shard_map/psum | solution.py:96
  1466.5 62.9 %psum.142 = f32[]{:T(128)} all-reduce(f32[]{:T(128)} %multiply_reduce_fusion), channel_id=1, replica_groups=mesh['dp'=4,'grid'=32] {'dp','grid'}, use_global_device_ids=true, to_apply=%region_36.37 | all-reduce | flops 1 | bytes 8 | tf_op jit(solution)/shard_map/psum | solution.py:88
  1596.1 63.0 %psum.143 = f32[]{:T(128)} all-reduce(f32[]{:T(128)} %fusion.84), channel_id=1, replica_groups=mesh['dp'=4,'grid'=32] {'dp','grid'}, use_global_device_ids=true, to_apply=%region_38.39 | all-reduce | flops 1 | bytes 8 | tf_op jit(solution)/shard_map/psum | solution.py:96
  (333 shorter events, 490.2 us)
Async XLA Ops:
  7.2 120.2 %reduce-scatter.2.cloned.1.call-start = ((), (), s32[]{:S(2)}) async-start(), calls=%async_computation.33 | async-start | bytes 8650752 | tf_op jit(solution)/shard_map/reduce_scatter | solution.py:72
  32.9 139.3 %all-reduce.4.cloned.1.call-start = ((), (), s32[]{:S(2)}) async-start(), calls=%async_computation.34 | async-start | bytes 1048576 | tf_op jit(solution)/shard_map/psum | solution.py:80
  177.6 18.8 %all-to-all-start.1 = ((f32[4,128,128]{2,0,1:T(4,128)}), f32[4,128,128]{2,0,1:T(4,128)S(1)}, u32[]{:S(2)}, u32[]{:S(2)}) async-start(f32[4,128,128]{2,0,1:T(4,128)} %copy.258), calls=%async_computation.2 | async-start | bytes 524288 | tf_op jit(solution)/shard_map/all_to_all | solution.py:35
  213.3 12.9 all-to-all-start.3
  375.6 14.2 all-to-all-start.5
  389.8 12.7 all-to-all-start.4
  406.7 12.7 all-to-all-start.7
  568.8 13.9 all-to-all-start.9
  582.6 12.7 all-to-all-start.8
  599.6 12.9 all-to-all-start.11
  612.4 12.7 all-to-all-start.10
  761.8 13.8 all-to-all-start.13
  775.6 13.1 all-to-all-start.12
  955.0 13.9 all-to-all-start.17
  998.4 12.9 all-to-all-start.18
  1148.0 13.8 all-to-all-start.21
  1161.8 13.1 all-to-all-start.20
  1179.1 12.7 all-to-all-start.23
  1341.2 13.8 all-to-all-start.25
  1371.9 12.7 all-to-all-start.27
  1384.6 12.9 all-to-all-start.26
  1534.2 13.8 all-to-all-start.29
  1548.1 12.9 all-to-all-start.28
  1566.2 13.4 all-to-all-start.31
  (14 other events, 199.9 us)
Sparse Core Ops, SparseCore 0:
  33.0 94.3 reduce-scatter.1
  130.4 41.7 all-reduce.3
where the time goes:
time: 1680 us; the launch traced here: 1670 us
  blocking collectives  945 us (56%)
  waiting for transfers between devices  373 us (22%)
  starting transfers between devices  139 us (8%)
  matrix products  114 us (7%)
  local copies, waits for them, and re-layouts  48.4 us (3%)
  between operations  36 us (2%)
    psum x8, blocking collectives, squares(): return lax.psum(jnp.sum(part * part), ('dp', 'grid'))  504 us
    psum x7, blocking collectives, body(): lax.psum(jnp.sum(own_rows(direction) * own_rows(image)), ('dp', 'grid'))  441 us
    dot_general x160, matrix products, along(): return jnp.einsum(form, field, table, precision=lax.Precision.HIGHEST)  107 us
    reduce_scatter x1, waiting for transfers between devices, body(): lax.psum_scatter(product.reshape(slab_rows * lax.axis_size('grid'), size)...  92.9 us
    all_to_all x8, waiting for transfers between devices, operate_slabs(): lax.all_to_all(mid_real, 'grid', split_axis=1, concat_axis=0, tiled=True)  64.5 us
    all_to_all x8, waiting for transfers between devices, operate_slabs(): lax.all_to_all(back_real, 'grid', split_axis=0, concat_axis=1, tiled=True)  64.3 us
    all_to_all x8, waiting for transfers between devices, operate_slabs(): lax.all_to_all(back_imag, 'grid', split_axis=0, concat_axis=1, tiled=True)  53.7 us
    all_to_all x8, waiting for transfers between devices, operate_slabs(): lax.all_to_all(mid_imag, 'grid', split_axis=1, concat_axis=0, tiled=True)  53.3 us
  transfers between devices with their start and end apart: 34, of which 34 were waited for; matrix products, arithmetic and copies ran while one was open for 3% of the time, Pallas kernels for 0%

commit v1 on v0

v1 whole, which is shorter than its diff:
```python
import functools

import jax
import jax.numpy as jnp
import numpy as np
from jax import lax
from jax.experimental import pallas as pl
from jax.experimental.pallas import tpu as pltpu
from jax.sharding import PartitionSpec as P

ITERS = 8
MOMENTS = 2 * ITERS + 1
LOW_LANE = 64
ALL = ("dp", "grid")
HIGHEST = lax.Precision.HIGHEST


def two_sum(a, b):
    s = a + b
    v = s - a
    return s, (a - (s - v)) + (b - v)


def quick_sum(a, b):
    s = a + b
    return s, b - (s - a)


def halves(a):
    c = a * 4097.0
    high = c - (c - a)
    return high, a - high


def two_prod(a, b, a_parts=None, b_parts=None):
    p = a * b
    ah, al = a_parts or halves(a)
    bh, bl = b_parts or halves(b)
    return p, ((ah * bh - p) + ah * bl + al * bh) + al * bl


def dd_add(a, b):
    s, e = two_sum(a[0], b[0])
    t, f = two_sum(a[1], b[1])
    s, e = quick_sum(s, e + t)
    return quick_sum(s, e + f)


def dd_mul(a, b):
    p, e = two_prod(a[0], b[0])
    return quick_sum(p, e + (a[0] * b[1] + a[1] * b[0]))


def dd_scale(a, factor):
    return a[0] * factor, a[1] * factor


def dd_neg(a):
    return -a[0], -a[1]


def dd_div(a, b):
    first = a[0] / b[0]
    rest = dd_add(a, dd_neg(dd_mul((first, jnp.zeros_like(first)), b)))
    second = rest[0] / b[0]
    rest = dd_add(rest, dd_neg(dd_mul((second, jnp.zeros_like(second)), b)))
    third = rest[0] / b[0]
    high, low = quick_sum(first, second)
    return quick_sum(high, low + third)


def dot(a, b):
    return jax.lax.dot_general(
        a, b, (((1,), (0,)), ((), ())), precision=HIGHEST, preferred_element_type=jnp.float32
    )


def owner_order(size, ndp):
    slots = size // ndp
    d = np.arange(size)
    return ndp * (d % slots) + d // slots


def dft_tables(size, ndp):
    index = np.arange(size)
    angle = 2.0 * np.pi * ((index[:, None] * index[None, :]) % size) / size
    cos, sin = np.cos(angle), np.sin(angle)
    order = owner_order(size, ndp)
    as_f32 = lambda a: np.ascontiguousarray(a, dtype=np.float32)
    return dict(
        lanes=as_f32(np.concatenate([cos, sin], 1)),
        own_rows=as_f32(np.concatenate([cos[order], sin[order]], 0)),
        own_cols=as_f32(np.concatenate([cos[:, order], sin[:, order]], 0)),
        back_rows=as_f32(np.concatenate([cos, sin], 0)),
        back_own=as_f32(np.concatenate([cos[:, order], sin[:, order]], 0)),
        mirror=as_f32(((index[:, None] + index[None, :]) % size) == 0),
    )


def plane_kernel(plane_ref, own_ref, mirrored_ref, lanes_ref, rows_ref, out_ref, sym_ref):
    size = plane_ref.shape[0]
    sym = (own_ref[...] + mirrored_ref[...]) * 0.5
    sym_ref[...] = sym
    low = jnp.min(jnp.min(sym, axis=0, keepdims=True), axis=1, keepdims=True)
    high = jnp.max(jnp.max(sym, axis=0, keepdims=True), axis=1, keepdims=True)
    first = dot(plane_ref[...], lanes_ref[...])
    both = dot(rows_ref[...], first)
    real = both[:size, :size] - both[size:, size:]
    imag = -(both[size:, :size] + both[:size, size:])
    out_ref[:, 0, :] = real
    out_ref[:, 1, :] = imag
    out_ref[:, 2, :] = jnp.broadcast_to(low, (size, size))
    out_ref[:, 3, :] = jnp.broadcast_to(high, (size, size))


def sublane_total(a):
    for shift in (4, 2, 1):
        a = dd_add(a, (pltpu.roll(a[0], shift, 0), pltpu.roll(a[1], shift, 0)))
    return a


def lane_total(a):
    for shift in (64, 32, 16, 8, 4, 2, 1):
        a = dd_add(a, (pltpu.roll(a[0], shift, 1), pltpu.roll(a[1], shift, 1)))
    return a


def moment_kernel(columns_ref, sym_ref, cols_ref, real_ref, imag_ref, scaled_ref, range_ref, send_ref):
    size = sym_ref.shape[0]
    low = jnp.min(jnp.min(columns_ref[:, 2, :], axis=0, keepdims=True), axis=1, keepdims=True)
    high = jnp.max(jnp.max(columns_ref[:, 3, :], axis=0, keepdims=True), axis=1, keepdims=True)
    half = jnp.maximum((high - low) * 0.5, high * 1e-4)
    half = jnp.broadcast_to(half, (1, size))
    centre = jnp.broadcast_to((high + low) * 0.5, (1, size)) / half
    range_ref[0:1, :] = half
    range_ref[1:2, :] = centre
    range_ref[2:8, :] = jnp.zeros((6, size), jnp.float32)
    given = jnp.concatenate([columns_ref[:, 0, :], columns_ref[:, 1, :]], axis=1)
    both = dot(cols_ref[...], given)
    real = both[:size, :size] + both[size:, size:]
    imag = both[:size, size:] - both[size:, :size]
    real_ref[...] = real
    imag_ref[...] = imag
    scaled = sym_ref[...] / half
    scaled_ref[...] = scaled
    power = real * real + imag * imag
    chunk = 32
    totals = [None] * MOMENTS
    for start in range(0, size, chunk):
        t = scaled[start : start + chunk] - centre
        p = power[start : start + chunk]
        p_parts = halves(p)
        t2 = t * 2.0
        t2_parts = halves(t2)
        zero = jnp.zeros_like(t)
        before, here = (jnp.ones_like(t), zero), (t, zero)
        for order in range(MOMENTS):
            value = before
            v_parts = halves(value[0])
            term, low_term = two_prod(value[0], p, v_parts, p_parts)
            term = (term, low_term + value[1] * p)
            rows = [(term[0][i : i + 8], term[1][i : i + 8]) for i in range(0, chunk, 8)]
            while len(rows) > 1:
                rows = [dd_add(rows[i], rows[i + 1]) for i in range(0, len(rows), 2)]
            totals[order] = rows[0] if totals[order] is None else dd_add(totals[order], rows[0])
            if order + 1 < MOMENTS:
                up, low_up = two_prod(here[0], t2, None, t2_parts)
                up, low_up = quick_sum(up, low_up + here[1] * t2)
                following = dd_add((up, low_up), dd_neg(before))
                before, here = here, following
    row = lax.broadcasted_iota(jnp.int32, (8, size), 0)
    lane = lax.broadcasted_iota(jnp.int32, (8, size), 1)
    out = jnp.zeros((8, size), jnp.float32)
    for base in range(0, MOMENTS, 8):
        high_rows = jnp.zeros((8, size), jnp.float32)
        low_rows = jnp.zeros((8, size), jnp.float32)
        for order in range(base, min(base + 8, MOMENTS)):
            total = sublane_total(totals[order])
            high_rows = jnp.where(row == order - base, total[0], high_rows)
            low_rows = jnp.where(row == order - base, total[1], low_rows)
        high_rows, low_rows = lane_total((high_rows, low_rows))
        out = jnp.where(lane == row + base, high_rows, out)
        out = jnp.where(lane == row + (base + LOW_LANE), low_rows, out)
    line = jnp.sum(out, axis=0, keepdims=True)
    send_ref[...] = jnp.broadcast_to(line, (size, size))


def lane_of(a, lane):
    pick = lambda v: jnp.broadcast_to(v[:, lane : lane + 1], v.shape)
    return pick(a[0]), pick(a[1])


def solve_kernel(sums_ref, range_ref, scaled_ref, real_ref, imag_ref, rows_ref, out_ref, gain_ref, *, scale):
    size = scaled_ref.shape[0]
    given = sums_ref[...]
    low = pltpu.roll(given, size - LOW_LANE, 1)
    rows = [(given[i : i + 8], low[i : i + 8]) for i in range(0, given.shape[0], 8)]
    while len(rows) > 1:
        rows = [dd_add(rows[i], rows[i + 1]) for i in range(0, len(rows), 2)]
    moments = sublane_total(rows[0])
    half = range_ref[0:1, :]
    centre = jnp.broadcast_to(range_ref[1:2, :], moments[0].shape)
    centre = (centre, jnp.zeros_like(centre))
    lane = lax.broadcasted_iota(jnp.int32, moments[0].shape, 1)
    resid, direct = moments, moments
    steps, turns = [], []
    decay = jnp.ones((1, size), jnp.float32)
    for k in range(ITERS):
        after = tuple(pltpu.roll(v, size - 1, 1) for v in direct)
        prior = tuple(pltpu.roll(v, 1, 1) for v in direct)
        prior = tuple(jnp.where(lane == 0, a, p) for a, p in zip(after, prior))
        image = dd_add(dd_mul(direct, centre), dd_scale(dd_add(after, prior), 0.5))
        alpha = dd_div(lane_of(resid, k), lane_of(image, k))
        fresh = dd_add(resid, dd_neg(dd_mul(alpha, image)))
        beta = dd_mul(alpha, dd_div(lane_of(fresh, k + 1), lane_of(resid, k)))
        beta = dd_scale(beta, -1.0 if k == 0 else -0.5)
        direct = dd_add(fresh, dd_mul(beta, direct))
        resid = fresh
        steps.append(alpha[0][0:1])
        turns.append(beta[0][0:1])
        decay = decay * beta[0][0:1]
    gain = lax.rsqrt(jnp.maximum(jnp.abs(decay), 1e-30)) / centre[0][0:1]
    gain_ref[...] = jnp.broadcast_to(gain, gain_ref.shape)
    scaled = scaled_ref[...]
    field = steps[0]
    solved = jnp.broadcast_to(field, scaled.shape)
    left = 1.0 - field * scaled
    toward = left + turns[0]
    for k in range(1, ITERS):
        solved = solved + steps[k] * toward
        left = left - steps[k] * (scaled * toward)
        if k + 1 < ITERS:
            toward = left + turns[k] * toward
    solved = solved * (scale / half)
    left = left * (gain * scale)
    real, imag = real_ref[...], imag_ref[...]
    back_real = solved * real - left * imag
    back_imag = solved * imag + left * real
    both = dot(rows_ref[...], jnp.concatenate([back_real, back_imag], axis=1))
    out_ref[0] = both[:size, :size] - both[size:, size:]
    out_ref[1] = both[:size, size:] + both[size:, :size]


def output_kernel(given_ref, gain_ref, own_ref, lanes_ref, field_ref, resid_ref):
    planes, size = field_ref.shape[0], field_ref.shape[1]
    wide = jnp.concatenate([given_ref[:, i, :] for i in range(2 * planes)], axis=1)
    both = dot(own_ref[...], wide)
    shrink = 1.0 / gain_ref[0:1, :]
    for j in range(planes):
        at = 2 * j * size
        real = both[:size, at : at + size] - both[size:, at + size : at + 2 * size]
        imag = both[:size, at + size : at + 2 * size] + both[size:, at : at + size]
        ends = dot(jnp.concatenate([real, imag], axis=0), lanes_ref[...])
        field_ref[j] = ends[:size, :size] - ends[size:, size:]
        resid_ref[j] = (ends[size:, :size] + ends[:size, size:]) * shrink


def call(kernel, name, shapes, *args):
    whole = pl.BlockSpec(memory_space=pltpu.VMEM)
    return pl.pallas_call(
        kernel,
        out_shape=[jax.ShapeDtypeStruct(s, jnp.float32) for s in shapes],
        in_specs=[whole] * len(args),
        out_specs=[whole] * len(shapes),
        name=name,
    )(*args)


def grid_sums(intensities, gridding, dest_slab, ngrid):
    nent, rows, size = intensities.shape
    slab_rows = gridding.shape[2]
    capacity = max(2, 2 * nent // ngrid)
    target = dest_slab[:, 0]
    member = (target[:, None] == jnp.arange(ngrid, dtype=jnp.int32)[None, :]).astype(jnp.int32)
    before = jnp.sum((jnp.cumsum(member, axis=0) - member) * member, axis=1)
    slot = target * capacity + before
    value_slots = jnp.zeros((ngrid * capacity, rows, size), intensities.dtype).at[slot].set(intensities)
    matrix_slots = jnp.zeros((ngrid * capacity, rows, slab_rows), gridding.dtype).at[slot].set(gridding)
    return lax.dot_general(
        matrix_slots.reshape(ngrid, capacity * rows, slab_rows),
        value_slots.reshape(ngrid, capacity * rows, size),
        (((1,), (1,)), ((0,), (0,))),
        preferred_element_type=jnp.float32,
    )


def body(intensities, gridding, dest_slab, spectral_weights):
    ngrid = lax.axis_size("grid")
    ndp = lax.axis_size("dp")
    size = intensities.shape[2]
    slab_rows = gridding.shape[2]
    planes = slab_rows // size
    count = ngrid * ndp
    table = dft_tables(size, ndp)

    pieces = jnp.moveaxis(spectral_weights[0], 1, 0)
    arrived = lax.all_to_all(pieces, "dp", 0, 0, tiled=True)
    own = jnp.sum(arrived, axis=0)
    flip = lambda w: jnp.roll(jnp.flip(w, (0, 1)), (1, 1), (0, 1))
    ky = owner_order(size, ndp)
    holder = np.argsort(ky)
    mirrored = lax.ppermute(flip(own), ALL, [(d, int(holder[(-ky[d]) % size])) for d in range(count)])

    product = grid_sums(intensities, gridding, dest_slab, ngrid)
    partial = lax.psum_scatter(product.reshape(slab_rows * ngrid, size), "grid", scatter_dimension=0, tiled=True)
    plane = lax.psum_scatter(partial, "dp", scatter_dimension=0, tiled=True)

    forward, sym = call(
        plane_kernel, "plane", [(size, 4, size), (size, size)],
        plane, own, mirrored, table["lanes"], table["own_rows"],
    )
    columns = lax.all_to_all(forward, ALL, 0, 0, tiled=True)
    square = (size, size)
    real, imag, scaled, ends, send = call(
        moment_kernel, "moments", [square, square, square, (8, size), square],
        columns, sym, table["own_cols"],
    )
    sums = lax.all_to_all(send.reshape(count, 1, size), ALL, 0, 0, tiled=True).reshape(count, size)
    back, gain = call(
        functools.partial(solve_kernel, scale=1.0 / size**3), "solve", [(2, size, size), (8, size)],
        sums, ends, scaled, real, imag, table["back_rows"],
    )
    spread = jnp.transpose(back.reshape(2, ngrid, planes, size), (1, 2, 0, 3)).reshape(1, ngrid, 2 * planes, size)
    spread = jnp.broadcast_to(spread, (ndp, ngrid, 2 * planes, size)).reshape(count, 2 * planes, size)
    given = lax.all_to_all(spread, ALL, 0, 0, tiled=True)
    return tuple(
        call(
            output_kernel, "planes_back", [(planes, size, size)] * 2,
            given, gain, table["back_own"], table["lanes"],
        )
    )


def solution(mesh):
    return jax.shard_map(
        body,
        mesh=mesh,
        in_specs=(
            P(("dp", "grid"), None, None),
            P(("dp", "grid"), None, None),
            P(("dp", "grid"), None),
            P("dp", None, "grid", None),
        ),
        out_specs=(P("grid", None, None), P("grid", None, None)),
        check_vma=False,
    )
```

time: 1680 us -> 227 us (0.14)
  blocking collectives: 945 us -> 63.5 us
  waiting for transfers between devices: 373 us -> 103 us
  starting transfers between devices: 139 us -> 4.4 us
  matrix products: 114 us -> 6.73 us
  local copies, waits for them, and re-layouts: 48.4 us -> 15.1 us
  between operations: 36 us -> 14.2 us
  Pallas kernels: 0 us -> 17.1 us
    psum x15 -> x0, blocking collectives: 945 us -> none  [the longest x8 504 us: squares(): return lax.psum(jnp.sum(part * part), ('dp', 'grid'))]
    all_to_all x32 -> x0, waiting for transfers between devices: 236 us -> none  [the longest x8 64.5 us: operate_slabs(): lax.all_to_all(mid_real, 'grid', split_axis=1, concat_axis=0, tiled=True)]
    all_to_all x32 -> x0, starting transfers between devices: 138 us -> none  [the longest x8 45.2 us: operate_slabs(): lax.all_to_all(mid_imag, 'grid', split_axis=1, concat_axis=0, tiled=True)]
    dot_general x161 -> x1, matrix products: 114 us -> 6.73 us  [grid_sums(): lax.dot_general(matrix_slots.reshape(ngrid, capacity * rows, slab_rows),...]
    all_to_all x0 -> x4, blocking collectives: none -> 63.5 us  [the longest x1 21 us: body(): columns = lax.all_to_all(forward, ALL, 0, 0, tiled=True)]
    psum x1 -> x0, waiting for transfers between devices: 44.8 us -> none  [body(): right_side = lax.psum(partial_value, 'dp').reshape(planes, size, size)]
    pallas_call x0 -> x4, Pallas kernels: none -> 17.1 us  [call(): pl.pallas_call(kernel, out_shape=[jax.ShapeDtypeStruct(s, jnp.float32) fo...]
    reduce_scatter x1 -> x2, waiting for transfers between devices: 92.9 us -> 98.5 us  [the longest x1 94.5 us: body(): lax.psum_scatter(product.reshape(slab_rows * ngrid, size), 'grid', scatte...]
  transfers between devices with their start and end apart: 34 -> 3, of which waited for: 34 -> 3; matrix products, arithmetic and copies ran while one was open for 3% -> 0% of each run, Pallas kernels for 0% -> 0%
where the time goes in v1:
time: 227 us; the launch traced here: 226 us
  waiting for transfers between devices  103 us (45%)
  blocking collectives  63.5 us (28%)
  Pallas kernels  17.1 us (8%)
  local copies, waits for them, and re-layouts  15.1 us (7%)
  between operations  14.2 us (6%)
  matrix products  6.73 us (3%)
  starting transfers between devices  4.4 us (2%)
  other arithmetic  2.66 us (1%)
    reduce_scatter x1, waiting for transfers between devices, body(): lax.psum_scatter(product.reshape(slab_rows * ngrid, size), 'grid', scatte...  94.5 us
    all_to_all x1, blocking collectives, body(): columns = lax.all_to_all(forward, ALL, 0, 0, tiled=True)  21 us
    all_to_all x1, blocking collectives, body(): given = lax.all_to_all(spread, ALL, 0, 0, tiled=True)  18.2 us
    pallas_call x4, Pallas kernels, call(): pl.pallas_call(kernel, out_shape=[jax.ShapeDtypeStruct(s, jnp.float32) fo...  17.1 us
    all_to_all x1, blocking collectives, body(): lax.all_to_all(send.reshape(count, 1, size), ALL, 0, 0, tiled=True)  15 us
    all_to_all x1, blocking collectives, body(): arrived = lax.all_to_all(pieces, 'dp', 0, 0, tiled=True)  9.28 us
    scatter x1, local copies, waits for them, and re-layouts, grid_sums(): jnp.zeros((ngrid * capacity, rows, slab_rows), gridding.dtype).at[slot]  8.64 us
    dot_general x1, matrix products, grid_sums(): lax.dot_general(matrix_slots.reshape(ngrid, capacity * rows, slab_rows),...  6.73 us
  transfers between devices with their start and end apart: 3, of which 3 were waited for; matrix products, arithmetic and copies ran while one was open for 0% of the time, Pallas kernels for 0%

profile of v1, /device:TPU:1, one launch (start us, length us, event | category | flops | bytes accessed | tf_op | source)
XLA Modules:
  0.0 226.1 jit_solution(14184805925726600176)
XLA Ops:
  7.2 0.9 fusion.1
  8.1 0.1 reduce_window_sum.11
  8.2 0.8 select_reduce_fusion
  9.0 0.7 fusion.2
  9.7 2.5 %broadcast_in_dim.16 = bf16[128,32,512]{2,1,0:T(8,128)(2,1)} broadcast(bf16[]{:T(256)} %constant.9.clone.1), dimensions={} | broadcast | bytes 4194306 | tf_op jit(solution)/shard_map/broadcast_in_dim | solution.py:278
  12.2 8.6 %scatter_fusion = bf16[128,32,512]{2,1,0:T(8,128)(2,1)} fusion(bf16[128,32,512]{2,1,0:T(8,128)(2,1)} %broadcast_in_dim.16, s32[64]{0:T(128)S(1)} %fusion.2, bf16[64,32,512]{2,1,0:T(8,128)(2,1)S(1)} %copy-done), kind=kCustom, calls=%fused_computation | custom fusion | bytes 6291712 | tf_op jit(solution)/shard_map/scatter | solution.py:278
  20.8 0.1 broadcast_in_dim.17
  21.0 2.5 %scatter_fusion.1 = bf16[128,32,128]{2,1,0:T(8,128)(2,1)S(1)} fusion(bf16[128,32,128]{2,1,0:T(8,128)(2,1)S(1)} %broadcast_in_dim.17, s32[64]{0:T(128)S(1)} %fusion.2, bf16[64,32,128]{2,1,0:T(8,128)(2,1)S(1)} %copy-done.2), kind=kCustom, calls=%fused_computation.1 | custom fusion | bytes 1573120 | tf_op jit(solution)/shard_map/scatter | solution.py:277
  23.5 6.7 %fusion.3 = f32[32,512,128]{2,1,0:T(8,128)} fusion(bf16[32,128,512]{2,1,0:T(8,128)(2,1)} %bitcast.27, bf16[32,128,128]{2,1,0:T(8,128)(2,1)S(1)} %bitcast.28), kind=kOutput, calls=%fused_computation.12 | convolution fusion | flops 536870912 | bytes 13631488 | tf_op jit(solution)/shard_map/dot_general | solution.py:279
  30.3 94.5 %reduce-scatter.3.cloned.1.call-done = f32[512,128]{1,0:T(8,128)} async-done(((f32[16384,128]{1,0:T(8,128)}), f32[512,128]{1,0:T(8,128)}) %reduce-scatter.3.cloned.1.call-update) | async-done | bytes 262160 | tf_op jit(solution)/shard_map/reduce_scatter | solution.py:305
  124.8 9.3 %all_to_all.20 = f32[4,128,128]{2,1,0:T(8,128)S(1)} all-to-all(f32[4,128,128]{2,1,0:T(8,128)S(1)} %bitcast.30), channel_id=1, replica_groups=mesh['dp'=4,'grid'=32] {'dp'}, dimensions={0} | all-to-all | bytes 524288 | tf_op jit(solution)/shard_map/all_to_all | solution.py:297
  134.2 0.1 slice.25
  134.3 0.1 slice.23
  134.6 4.3 %collective-permute-start = (f32[128,128]{1,0:T(8,128)S(1)}, f32[128,128]{1,0:T(8,128)S(1)}, u32[]{:S(2)}, u32[]{:S(2)}) collective-permute-start(f32[128,128]{1,0:T(8,128)S(1)} %fusion), channel_id=1, source_target_pairs={{0,0},{1,31},{2,30},{3,29},{4,28},{5,27},{6,26},{7,25},{8,24},{9,2... | collective-permute-start | bytes 196616 | tf_op jit(solution)/shard_map/ppermute | solution.py:302
  138.9 4.0 %collective-permute-done.mirrored_ref = f32[128,128]{1,0:T(8,128)S(1)} collective-permute-done((f32[128,128]{1,0:T(8,128)S(1)}, f32[128,128]{1,0:T(8,128)S(1)}, u32[]{:S(2)}, u32[]{:S(2)}) %collective-permute-start) | collective-permute-done | bytes 65568 | tf_op jit(solution)/shard_map/ppermute | solution.py:302
  142.9 4.0 %reduce-scatter.5.cloned.1.call-done.plane_ref = f32[128,128]{1,0:T(8,128)} async-done(((f32[512,128]{1,0:T(8,128)}), f32[128,128]{1,0:T(8,128)}) %reduce-scatter.5.cloned.1.call-update) | async-done | bytes 65552 | tf_op jit(solution)/shard_map/reduce_scatter | solution.py:306
  147.0 2.6 %plane.1 = (f32[128,4,128]{2,1,0:T(4,128)}, f32[128,128]{1,0:T(8,128)}) custom-call(f32[128,128]{1,0:T(8,128)} %reduce-scatter.5.cloned.1.call-done.plane_ref, f32[128,128]{1,0:T(8,128)} %copy-done.1, f32[128,128]{1,0:T(8,128)} %copy-done.4, f32[128,256]{1,0:T(8,128)} %constant.24.clone.lanes_ref, f32[256,128]{1,0:T(8,128)} %constant.25.clone.rows_ref), custom_call_target="tpu_custom_call" | custom-call | tf_op jit(solution)/shard_map/plane/pallas_call | solution.py:260
  149.6 21.0 %all_to_all.21.columns_ref = f32[128,4,128]{2,1,0:T(4,128)} all-to-all(f32[128,4,128]{2,1,0:T(4,128)} %get-tuple-element.11), channel_id=1, replica_groups=mesh['dp'=4,'grid'=32] {'dp','grid'}, dimensions={0} | all-to-all | bytes 524288 | tf_op jit(solution)/shard_map/all_to_all | solution.py:312
  170.6 5.2 %moments.1 = (f32[128,128]{1,0:T(8,128)}, f32[128,128]{1,0:T(8,128)}, f32[128,128]{1,0:T(8,128)}, f32[8,128]{1,0:T(8,128)}, f32[128,128]{1,0:T(8,128)}) custom-call(f32[128,4,128]{2,1,0:T(4,128)} %all_to_all.21.columns_ref, f32[128,128]{1,0:T(8,128)} %get-tuple-element.12.sym_ref, f32[256,128]{1,0:T(8,128)} %constant.26.clone.cols_ref.own_ref), custom_call_target="tpu_custom_call" | custom-call | tf_op jit(solution)/shard_map/moments/pallas_call | solution.py:260
  175.8 15.0 %all_to_all.22 = f32[128,1,128]{2,1,0:T(1,128)} all-to-all(f32[128,1,128]{2,1,0:T(1,128)} %bitcast.34), channel_id=1, replica_groups=mesh['dp'=4,'grid'=32] {'dp','grid'}, dimensions={0} | all-to-all | bytes 131072 | tf_op jit(solution)/shard_map/all_to_all | solution.py:318
  190.8 5.4 %solve.1 = (f32[2,128,128]{2,1,0:T(8,128)}, f32[8,128]{1,0:T(8,128)}) custom-call(f32[128,128]{1,0:T(8,128)} %bitcast.32, f32[8,128]{1,0:T(8,128)} %get-tuple-element.14.range_ref, f32[128,128]{1,0:T(8,128)} %get-tuple-element.15.scaled_ref, f32[128,128]{1,0:T(8,128)} %get-tuple-element.16.real_ref, f32[128,128]{1,0:T(8,128)} %get-tuple-element.17.imag_ref, ...), custom_call_target="tpu_custom_call" | custom-call | tf_op jit(solution)/shard_map/solve/pallas_call | solution.py:260
  196.2 0.9 copy.17
  197.2 18.2 %all_to_all.23.given_ref = f32[128,8,128]{2,1,0:T(8,128)} all-to-all(f32[128,8,128]{2,1,0:T(8,128)S(1)} %bitcast.29), channel_id=1, replica_groups=mesh['dp'=4,'grid'=32] {'dp','grid'}, dimensions={0} | all-to-all | bytes 1048576 | tf_op jit(solution)/shard_map/all_to_all | solution.py:325
  215.4 3.9 %planes_back.1 = (f32[4,128,128]{2,1,0:T(8,128)}, f32[4,128,128]{2,1,0:T(8,128)}) custom-call(f32[128,8,128]{2,1,0:T(8,128)} %all_to_all.23.given_ref, f32[8,128]{1,0:T(8,128)} %get-tuple-element.19.gain_ref, f32[256,128]{1,0:T(8,128)} %constant.26.clone.cols_ref.own_ref, f32[128,256]{1,0:T(8,128)} %constant.24.clone.lanes_ref), custom_call_target="tpu_custom_call" | custom-call | tf_op jit(solution)/shard_map/planes_back/pallas_call | solution.py:260
  (22 shorter events, 0.5 us)
Async XLA Ops:
  7.2 5.0 %copy-start = (bf16[64,32,512]{2,1,0:T(8,128)(2,1)S(1)}, bf16[64,32,512]{2,1,0:T(8,128)(2,1)}, u32[]{:S(2)}) copy-start(bf16[64,32,512]{2,1,0:T(8,128)(2,1)} %param.10) | copy-start | bytes 6291460
  7.2 117.6 %reduce-scatter.3.cloned.1.call-start = ((), (), s32[]{:S(2)}) async-start(), calls=%async_computation.6 | async-start | bytes 8650752 | tf_op jit(solution)/shard_map/reduce_scatter | solution.py:305
  12.2 8.8 %copy-start.2 = (bf16[64,32,128]{2,1,0:T(8,128)(2,1)S(1)}, bf16[64,32,128]{2,1,0:T(8,128)(2,1)}, u32[]{:S(2)}) copy-start(bf16[64,32,128]{2,1,0:T(8,128)(2,1)} %param.9) | copy-start | bytes 1572868
  30.2 94.6 %copy-start.3 = (f32[1,128,4,128]{3,2,1,0:T(4,128)S(1)}, f32[1,128,4,128]{3,2,1,0:T(4,128)}, u32[]{:S(2)}) copy-start(f32[1,128,4,128]{3,2,1,0:T(4,128)} %param.12) | copy-start | bytes 786436
  30.3 116.7 %reduce-scatter.5.cloned.1.call-start = ((), (), s32[]{:S(2)}) async-start(), calls=%async_computation.7 | async-start | bytes 327680 | tf_op jit(solution)/shard_map/reduce_scatter | solution.py:306
  134.1 12.8 %copy-start.1 = (f32[128,128]{1,0:T(8,128)}, f32[128,128]{1,0:T(8,128)S(1)}, u32[]{:S(2)}) copy-start(f32[128,128]{1,0:T(8,128)S(1)} %reduce_sum.22.own_ref) | copy-start | bytes 196612
  134.6 8.3 %collective-permute-start = (f32[128,128]{1,0:T(8,128)S(1)}, f32[128,128]{1,0:T(8,128)S(1)}, u32[]{:S(2)}, u32[]{:S(2)}) collective-permute-start(f32[128,128]{1,0:T(8,128)S(1)} %fusion), channel_id=1, source_target_pairs={{0,0},{1,31},{2,30},{3,29},{4,28},{5,27},{6,26},{7,25},{8,24},{9,2... | collective-permute-start | bytes 196616 | tf_op jit(solution)/shard_map/ppermute | solution.py:302
  142.9 4.1 %copy-start.4 = (f32[128,128]{1,0:T(8,128)}, f32[128,128]{1,0:T(8,128)S(1)}, u32[]{:S(2)}) copy-start(f32[128,128]{1,0:T(8,128)S(1)} %collective-permute-done.mirrored_ref) | copy-start | bytes 196612
Sparse Core Ops, SparseCore 0:
  30.4 94.3 reduce-scatter.2
  127.1 19.7 reduce-scatter.4
